TPU v7x, 512 devices: a whole 4x4x16 slice. The times are simulated.
512 devices in a mesh: ctx: 32 (over x, y, core), exp: 16 (over z).
Axes of the slice: x: 4, y: 4, z: 16, core: 2. Of those that a mesh axis runs over, the one named last changes fastest.
Arguments:
- residual: bfloat16 [4096, 2048], P('ctx', 'exp'), may hold values from -60 to 60
- ssd_input: bfloat16 [4096, 2048], P('ctx', 'exp'), may hold values from -6 to 6
- state_in: bfloat16 [4096, 128], P('ctx'), may hold values from -0.015625 to 0.015625
- state_out: bfloat16 [4096, 128], P('ctx'), may hold values from -6 to 6
- log_decay: float32 [4096, 64], P('ctx', 'exp'), may hold values from -1 to 0
- skip_gain: float32 [64], P('exp'), may hold values from 0.5 to 1.5
- norm_gain: float32 [2048], P('exp'), may hold values from 0.1 to 1.9
- route_weight: float32 [4096, 2], P('ctx'), may hold values from 0.2 to 1
- expert_ids: int32 [4096, 2], P('ctx'), may hold values from 0 to 15, all different within a row; in each aligned block of 128 rows (0 to 127, 128 to 255, ...) at most 16 rows name the same one
- weight_in: bfloat16 [16, 2048, 8192], P('exp', None, 'ctx'), may hold values from -0.125 to 0.125
- weight_down: bfloat16 [16, 8192, 2048], P('exp', 'ctx'), may hold values from -0.125 to 0.125
- out_grad: bfloat16 [4096, 2048], P('ctx', 'exp'), may hold values from -6 to 6
Outputs:
- block_out: bfloat16 [4096, 2048], P('ctx', 'exp')
- grad_residual: bfloat16 [4096, 2048], P('ctx', 'exp')
- grad_input: bfloat16 [4096, 2048], P('ctx', 'exp')
- grad_weight_in: bfloat16 [16, 2048, 8192], P('exp', None, 'ctx')
- grad_weight_down: bfloat16 [16, 8192, 2048], P('exp', 'ctx')
Inputs may be any that keep to these rules, and one draw needn't show every extreme that they name: `expert_ids`: the two experts of a token differ; in each aligned block of 128 rows (the tokens of one index of ctx) every expert is named by exactly 16 rows.
All inputs are finite; a program needn't handle non-finite values.
Results may differ from a plain program's by a relative error of at most 0.015.
Values may be sent and summed in bfloat16 or wider, within the bound.
No kernel may reach another device: no remote copies, remote signals or barrier semaphores. Data moves between devices by JAX's collectives and lax.ppermute only.
A program may use at most 64 MiB of HBM per device.

v0:
```python
import jax
import jax.numpy as jnp
from jax import lax
from jax.sharding import PartitionSpec as P

D = 2048
epsilon = 1e-05
highest = lax.Precision.HIGHEST


def carried_in(value, axis, combine, identity, reverse):
    peers, index = (lax.axis_size(axis), lax.axis_index(axis))
    everything = jax.tree.map(
        lambda part, kind: lax.all_gather(part.astype(kind), axis),
        value,
        (jnp.bfloat16, jnp.bfloat16),
    )
    start = jax.tree.map(
        lambda part, zero: jnp.broadcast_to(jnp.asarray(zero, part.dtype), part.shape),
        value,
        identity,
    )

    def step(k, before):
        at = peers - 1 - k if reverse else k
        reached = at > index if reverse else at < index
        new = combine(
            before, jax.tree.map(lambda part, own: part[at].astype(own.dtype), everything, value)
        )
        return jax.tree.map(lambda a, b: jnp.where(reached, a, b), new, before)

    return lax.fori_loop(0, peers, step, start)


def carry_state(earlier, later):
    return (earlier[0] * later[0], later[0][:, None, None] * earlier[1] + later[1])


def block_mixing(log_decay, state_in_wide, state_out_wide):
    cumulative = jnp.cumsum(log_decay, axis=0)
    inner_state = jnp.dot(state_out_wide, state_in_wide.T, precision=highest)
    location_list = jnp.arange(cumulative.shape[0])
    causal = location_list[:, None] >= location_list[None, :]
    gap_log = cumulative[:, None, :] - cumulative[None, :, :]
    weights = inner_state[:, :, None] * jnp.exp(jnp.where(causal[:, :, None], gap_log, -jnp.inf))
    return (cumulative, weights)


def collect_routes(dispatch_table, returned):
    flattened = returned.reshape(-1, returned.shape[2])
    routed = lax.dot_general(
        dispatch_table, flattened, (((0,), (0,)), ((), ())), preferred_element_type=jnp.float32
    )
    return routed.reshape(-1, 2, flattened.shape[1])


def body(
    residual,
    ssd_input,
    state_in,
    state_out,
    log_decay,
    skip_gain,
    norm_gain,
    route_weight,
    expert_ids,
    weight_in,
    weight_down,
    out_grad,
):
    tokens_here = residual.shape[0]
    heads_here = log_decay.shape[1]
    feature_width = residual.shape[1]
    head_width = feature_width // heads_here
    exp_count = lax.axis_size("exp")
    capacity = 2 * tokens_here // exp_count
    state_in_wide = state_in.astype(jnp.float32)
    state_out_wide = state_out.astype(jnp.float32)
    cumulative, weights = block_mixing(log_decay, state_in_wide, state_out_wide)
    head_input = ssd_input.astype(jnp.float32).reshape(tokens_here, heads_here, head_width)
    ending = cumulative[-1]
    tail_decay = jnp.exp(ending[None, :] - cumulative)
    block_state = jnp.einsum(
        "sh,sn,shp->hnp", tail_decay, state_in_wide, head_input, precision=highest
    )
    block_decay = jnp.exp(ending)
    identity = (jnp.ones_like(block_decay), jnp.zeros_like(block_state))
    incoming = carried_in((block_decay, block_state), "ctx", carry_state, identity, False)[1]
    ssd_out = jnp.einsum("tsh,shp->thp", weights, head_input, precision=highest)
    ssd_out = ssd_out + jnp.exp(cumulative)[:, :, None] * jnp.einsum(
        "tn,hnp->thp", state_out_wide, incoming, precision=highest
    )
    ssd_out = ssd_out + skip_gain[None, :, None] * head_input
    mixed = (residual.astype(jnp.float32) + ssd_out.reshape(tokens_here, feature_width)).astype(
        jnp.bfloat16
    )
    mixed_wide = mixed.astype(jnp.float32)
    square_sum = lax.psum(jnp.sum(mixed_wide * mixed_wide, axis=1), "exp")
    inv_rms = lax.rsqrt(square_sum / D + epsilon)[:, None]
    normed = (mixed_wide * inv_rms * norm_gain[None, :]).astype(jnp.bfloat16)
    route_ids = expert_ids.reshape(-1)
    onehot = (route_ids[:, None] == jnp.arange(exp_count)[None, :]).astype(jnp.int32)
    before = jnp.cumsum(onehot, axis=0) - onehot
    slot_index = jnp.sum(before * onehot, axis=1)
    target = route_ids * capacity + slot_index
    dispatch_table = (jnp.arange(exp_count * capacity)[:, None] == target[None, :]).astype(
        jnp.bfloat16
    )
    route_rows = jnp.repeat(normed, 2, axis=0)
    out_grad_wide = out_grad.astype(jnp.float32)
    route_cot = (route_weight.reshape(-1)[:, None] * jnp.repeat(out_grad_wide, 2, axis=0)).astype(
        jnp.bfloat16
    )
    spread_rows = (
        jnp.dot(dispatch_table, route_rows, preferred_element_type=jnp.float32)
        .astype(jnp.bfloat16)
        .reshape(exp_count, capacity, feature_width)
    )
    spread_cot = (
        jnp.dot(dispatch_table, route_cot, preferred_element_type=jnp.float32)
        .astype(jnp.bfloat16)
        .reshape(exp_count, capacity, feature_width)
    )
    arrived_rows, arrived_cot = (
        lax.all_to_all(spread_rows, "exp", split_axis=0, concat_axis=2, tiled=True),
        lax.all_to_all(spread_cot, "exp", split_axis=0, concat_axis=2, tiled=True),
    )
    expert_rows, cot_rows = (
        lax.all_gather(arrived_rows[0], "ctx", axis=0, tiled=True),
        lax.all_gather(arrived_cot[0], "ctx", axis=0, tiled=True),
    )
    matrix_in = weight_in[0]
    matrix_down = weight_down[0]
    hidden = jnp.dot(expert_rows, matrix_in, preferred_element_type=jnp.float32)
    activated = jax.nn.silu(hidden).astype(jnp.bfloat16)
    row_piece = activated
    out_rows = lax.psum_scatter(
        jnp.dot(row_piece, matrix_down, preferred_element_type=jnp.float32).astype(jnp.bfloat16),
        "ctx",
        scatter_dimension=0,
        tiled=True,
    )
    returned = lax.all_to_all(out_rows[None], "exp", split_axis=2, concat_axis=0, tiled=True)
    routed = collect_routes(dispatch_table, returned)
    expert_mix = jnp.sum(routed * route_weight[:, :, None], axis=1)
    block_out = (mixed_wide + expert_mix).astype(jnp.bfloat16)
    d_act = lax.dot_general(
        cot_rows, matrix_down, (((1,), (1,)), ((), ())), preferred_element_type=jnp.float32
    )
    sigmoid_h = jax.nn.sigmoid(hidden)
    d_hidden = (d_act * sigmoid_h * (1.0 + hidden * (1.0 - sigmoid_h))).astype(jnp.bfloat16)
    grad_down = lax.dot_general(
        activated, cot_rows, (((0,), (0,)), ((), ())), preferred_element_type=jnp.float32
    )
    grad_in = lax.dot_general(
        expert_rows, d_hidden, (((0,), (0,)), ((), ())), preferred_element_type=jnp.float32
    )
    row_piece = d_hidden
    d_rows = lax.psum_scatter(
        lax.dot_general(
            row_piece, matrix_in, (((1,), (1,)), ((), ())), preferred_element_type=jnp.float32
        ).astype(jnp.bfloat16),
        "ctx",
        scatter_dimension=0,
        tiled=True,
    )
    returned_grads = lax.all_to_all(d_rows[None], "exp", split_axis=2, concat_axis=0, tiled=True)
    d_normed = jnp.sum(collect_routes(dispatch_table, returned_grads), axis=1)
    scaled = norm_gain[None, :] * d_normed
    dot_terms = lax.psum(jnp.sum(scaled * mixed_wide, axis=1), "exp")[:, None]
    d_mixed = (
        out_grad_wide + inv_rms * scaled - mixed_wide * inv_rms * inv_rms * inv_rms * dot_terms / D
    )
    head_grad = d_mixed.reshape(tokens_here, heads_here, head_width)
    grad_heads = jnp.einsum("tsh,thp->shp", weights, head_grad, precision=highest)
    lead_decay = jnp.exp(cumulative)
    block_cot = jnp.einsum(
        "th,tn,thp->hnp", lead_decay, state_out_wide, head_grad, precision=highest
    )
    later_state = carried_in((block_decay, block_cot), "ctx", carry_state, identity, True)[1]
    grad_heads = grad_heads + tail_decay[:, :, None] * jnp.einsum(
        "sn,hnp->shp", state_in_wide, later_state, precision=highest
    )
    grad_heads = grad_heads + skip_gain[None, :, None] * head_grad
    grad_input = grad_heads.reshape(tokens_here, feature_width).astype(jnp.bfloat16)
    return (
        block_out,
        d_mixed.astype(jnp.bfloat16),
        grad_input,
        grad_in.astype(jnp.bfloat16)[None],
        grad_down.astype(jnp.bfloat16)[None],
    )


def solution(mesh):
    placed = (
        P("ctx", "exp"),
        P("ctx", "exp"),
        P("ctx", None),
        P("ctx", None),
        P("ctx", "exp"),
        P("exp"),
        P("exp"),
        P("ctx", None),
        P("ctx", None),
        P("exp", None, "ctx"),
        P("exp", "ctx", None),
        P("ctx", "exp"),
    )
    return jax.shard_map(
        body,
        mesh=mesh,
        in_specs=placed,
        out_specs=(
            P("ctx", "exp"),
            P("ctx", "exp"),
            P("ctx", "exp"),
            P("exp", None, "ctx"),
            P("exp", "ctx", None),
        ),
        check_vma=False,
    )
```

profile of v0, /device:TPU:1, one launch (start us, length us, event | category | flops | bytes accessed | tf_op | source)
XLA Modules:
  0.0 650.2 jit_solution(7748751069555235195)
XLA Ops:
  12.9 24.1 %all-gather.2 = bf16[32,1,4]{2,1,0:T(2,128)(2,1)S(1)} all-gather(bf16[1,1,4]{2,1,0:T(2,128)(2,1)S(1)} %get-tuple-element.356), channel_id=1, replica_groups=mesh['ctx'=32,'exp'=16] {'ctx'}, dimensions={0}, use_global_device_ids=true | all-gather | bytes 264 | tf_op jit(solution)/shard_map/all_gather | solution.py:14
  38.3 37.0 %all-gather.12.cloned.1.call-done = bf16[128,128,32]{1,2,0:T(8,128)(2,1)} async-done(((bf16[4,128,32]{1,2,0:T(8,128)(2,1)}), bf16[128,128,32]{1,2,0:T(8,128)(2,1)}) %all-gather.12.cloned.1.call-update) | async-done | bytes 1048592 | tf_op jit(solution)/shard_map/all_gather | solution.py:14
  75.3 33.7 %while.30 = (s32[]{:T(128)}, f32[4,128,32]{2,1,0:T(8,128)S(1)}, s32[]{:T(128)}, bf16[32,4]{1,0:T(8,128)(2,1)S(1)}, bf16[32,4,128,32]{2,3,1,0:T(8,128)(2,1)}, /*index=5*/s32[]{:T(128)}, s32[]{:T(128)}) while((s32[]{:T(128)}, f32[4,128,32]{2,1,0:T(8,128)S(1)}, s32[]{:T(128)}, bf16[32,4]{1,0:T(8,128)(2,1)S(1)}, ...), condition=%wide.region_2.3_spmd.clone, body=%wide.region_1.2_spmd.clone.sunk | while | flops 81928 | bytes 295065 | solution.py:32
  110.1 24.8 %psum.14 = f32[128]{0:T(128)S(1)} all-reduce(f32[128]{0:T(128)S(1)} %get-tuple-element.351), channel_id=1, replica_groups=mesh['ctx'=32,'exp'=16] {'exp'}, use_global_device_ids=true, to_apply=%region_7.8 | all-reduce | flops 128 | bytes 1024 | tf_op jit(solution)/shard_map/psum | solution.py:98
  135.2 19.0 %all_to_all.60 = bf16[16,16,128]{2,1,0:T(8,128)(2,1)S(1)} all-to-all(bf16[16,16,128]{2,1,0:T(8,128)(2,1)S(1)} %bitcast.189), channel_id=1, replica_groups=mesh['ctx'=32,'exp'=16] {'exp'}, dimensions={0} | all-to-all | bytes 131072 | tf_op jit(solution)/shard_map/all_to_all | solution.py:125
  155.6 14.2 %all_to_all.61 = bf16[16,16,128]{2,1,0:T(8,128)(2,1)S(1)} all-to-all(bf16[16,16,128]{2,1,0:T(8,128)(2,1)S(1)} %bitcast.168), channel_id=1, replica_groups=mesh['ctx'=32,'exp'=16] {'exp'}, dimensions={0} | all-to-all | bytes 131072 | tf_op jit(solution)/shard_map/all_to_all | solution.py:126
  170.6 42.3 %all-gather.8.cloned.1.call-done = bf16[512,2048]{1,0:T(8,128)(2,1)} async-done(((bf16[16,2048]{1,0:T(8,128)(2,1)}), bf16[512,2048]{1,0:T(8,128)(2,1)}) %all-gather.8.cloned.1.call-update) | async-done | bytes 2097168 | tf_op jit(solution)/shard_map/all_gather | solution.py:129
  212.9 2.3 fusion.19
  215.2 2.1 convolution_convert_fusion.1
  217.6 57.4 %all-gather.10.cloned.1.call-done = bf16[512,2048]{1,0:T(8,128)(2,1)} async-done(((bf16[16,2048]{1,0:T(8,128)(2,1)}), bf16[512,2048]{1,0:T(8,128)(2,1)}) %all-gather.10.cloned.1.call-update) | async-done | bytes 2097168 | tf_op jit(solution)/shard_map/all_gather | solution.py:130
  274.9 2.4 fusion.5
  277.3 2.1 convolution_convert_fusion
  279.4 99.2 %reduce-scatter.3.cloned.1.call-done = bf16[16,2048]{1,0:T(8,128)(2,1)} async-done(((bf16[512,2048]{1,0:T(8,128)(2,1)}), bf16[16,2048]{1,0:T(8,128)(2,1)}) %reduce-scatter.3.cloned.1.call-update) | async-done | bytes 65552 | tf_op jit(solution)/shard_map/reduce_scatter | solution.py:137
  378.6 2.0 copy.104
  381.1 11.5 %reduce.3 = bf16[2048,16]{1,0:T(8,128)(2,1)S(1)} reduce(bf16[2048,1,16]{2,1,0:T(2,128)(2,1)S(1)} %bitcast.163, bf16[]{:T(256)} %broadcast.81), dimensions={1}, to_apply=%bitcast.131.reduce_sub_computation | reduce | bytes 131074
  393.8 12.0 %all-to-all-start.1 = ((bf16[16,2,1024]{2,1,0:T(2,128)(2,1)}), bf16[16,2,1024]{2,1,0:T(2,128)(2,1)S(1)}, u32[]{:S(2)}, u32[]{:S(2)}) async-start(bf16[16,2,1024]{2,1,0:T(2,128)(2,1)} %reshape.206), calls=%async_computation.2 | async-start | bytes 131072 | tf_op jit(solution)/shard_map/all_to_all | solution.py:143
  405.8 78.6 %reduce-scatter.5.cloned.1.call-done = bf16[16,2048]{1,0:T(8,128)(2,1)} async-done(((bf16[512,2048]{1,0:T(8,128)(2,1)}), bf16[16,2048]{1,0:T(8,128)(2,1)}) %reduce-scatter.5.cloned.1.call-update) | async-done | bytes 65552 | tf_op jit(solution)/shard_map/reduce_scatter | solution.py:159
  486.4 11.5 %reduce.2 = bf16[2048,16]{1,0:T(8,128)(2,1)S(1)} reduce(bf16[2048,1,16]{2,1,0:T(2,128)(2,1)S(1)} %bitcast.164, bf16[]{:T(256)} %broadcast.81), dimensions={1}, to_apply=%bitcast.133.reduce_sub_computation | reduce | bytes 131074
  499.1 12.0 %all-to-all-start.3 = ((bf16[16,2,1024]{2,1,0:T(2,128)(2,1)}), bf16[16,2,1024]{2,1,0:T(2,128)(2,1)S(1)}, u32[]{:S(2)}, u32[]{:S(2)}) async-start(bf16[16,2,1024]{2,1,0:T(2,128)(2,1)} %reshape.208), calls=%async_computation.5 | async-start | bytes 131072 | tf_op jit(solution)/shard_map/all_to_all | solution.py:167
  512.9 9.8 %all-to-all-done.3 = bf16[16,2,1024]{2,1,0:T(2,128)(2,1)S(1)} async-done(((bf16[16,2,1024]{2,1,0:T(2,128)(2,1)}), bf16[16,2,1024]{2,1,0:T(2,128)(2,1)S(1)}, u32[]{:S(2)}, u32[]{:S(2)}) %all-to-all-start.3) | async-done | bytes 65568 | tf_op jit(solution)/shard_map/all_to_all | solution.py:167
  524.7 21.7 %psum.15 = f32[128]{0:T(128)S(1)} all-reduce(f32[128]{0:T(128)S(1)} %fusion.44), channel_id=1, replica_groups=mesh['ctx'=32,'exp'=16] {'exp'}, use_global_device_ids=true, to_apply=%region_13.14 | all-reduce | flops 128 | bytes 1024 | tf_op jit(solution)/shard_map/psum | solution.py:170
  548.1 3.5 fusion.2
  553.4 54.5 %all-gather.14.cloned.1.call-done = bf16[128,128,32]{1,2,0:T(8,128)(2,1)} async-done(((bf16[4,128,32]{1,2,0:T(8,128)(2,1)}), bf16[128,128,32]{1,2,0:T(8,128)(2,1)}) %all-gather.14.cloned.1.call-update) | async-done | bytes 1048592 | tf_op jit(solution)/shard_map/all_gather | solution.py:14
  607.9 33.9 %while.31 = (s32[]{:T(128)}, f32[4,128,32]{2,1,0:T(8,128)S(1)}, s32[]{:T(128)}, bf16[32,4]{1,0:T(8,128)(2,1)S(1)}, bf16[32,4,128,32]{2,3,1,0:T(8,128)(2,1)}, /*index=5*/s32[]{:T(128)}, s32[]{:T(128)}, s32[]{:T(128)}, s32[]{:T(128)}) while((s32[]{:T(128)}, f32[4,128,32]{2,1,0:T(8,128)S(1)}, s32[]{:T(128)}, ...), condition=%wide.region_15.16_spmd.clone, body=%wide.region_14.15_spmd.clone.sunk | while | flops 81932 | bytes 295127 | solution.py:32
  (360 shorter events, 89.0 us)
Async XLA Ops:
  7.2 208.0 %copy-start = (bf16[1,256,2048]{2,1,0:T(8,128)(2,1)S(1)}, bf16[1,256,2048]{2,1,0:T(8,128)(2,1)}, u32[]{:S(2)}) copy-start(bf16[1,256,2048]{2,1,0:T(8,128)(2,1)} %param.26) | copy-start | bytes 3145732
  7.2 68.1 %all-gather.12.cloned.1.call-start = ((), (), s32[]{:S(2)}) async-start(), calls=%async_computation.10 | async-start | bytes 1081344 | tf_op jit(solution)/shard_map/all_gather | solution.py:14
  10.8 202.0 %all-gather.8.cloned.1.call-start = ((), (), s32[]{:S(2)}) async-start(), calls=%async_computation.6 | async-start | bytes 2162688 | tf_op jit(solution)/shard_map/all_gather | solution.py:129
  75.3 33.8 %copy-start.3 = (bf16[128,128]{1,0:T(8,128)(2,1)S(1)}, bf16[128,128]{1,0:T(8,128)(2,1)}, u32[]{:S(2)}) copy-start(bf16[128,128]{1,0:T(8,128)(2,1)} %param.19) | copy-start | bytes 98308
  75.3 34.2 %copy-start.9 = (f32[4]{0:T(128)S(1)}, f32[4]{0:T(128)}, u32[]{:S(2)}) copy-start(f32[4]{0:T(128)} %param.21) | copy-start | bytes 52
  75.3 34.7 %copy-start.5 = (bf16[128,128]{1,0:T(8,128)(2,1)S(1)}, bf16[128,128]{1,0:T(8,128)(2,1)}, u32[]{:S(2)}) copy-start(bf16[128,128]{1,0:T(8,128)(2,1)} %param.16) | copy-start | bytes 98308
  75.3 59.6 %copy-start.6 = (f32[128]{0:T(128)S(1)}, f32[128]{0:T(128)}, u32[]{:S(2)}) copy-start(f32[128]{0:T(128)} %param.22) | copy-start | bytes 1540
  75.3 79.7 %copy-start.7 = (f32[128,2]{0,1:T(2,128)S(1)}, f32[128,2]{0,1:T(2,128)}, u32[]{:S(2)}) copy-start(f32[128,2]{0,1:T(2,128)} %param.23) | copy-start | bytes 3076
  75.3 80.0 %copy-start.4 = (bf16[128,128]{1,0:T(8,128)(2,1)S(1)}, bf16[128,128]{1,0:T(8,128)(2,1)}, u32[]{:S(2)}) copy-start(bf16[128,128]{1,0:T(8,128)(2,1)} %param.27) | copy-start | bytes 98308
  109.0 103.8 %copy-start.1 = (bf16[1,2048,256]{2,1,0:T(8,128)(2,1)S(1)}, bf16[1,2048,256]{2,1,0:T(8,128)(2,1)}, u32[]{:S(2)}) copy-start(bf16[1,2048,256]{2,1,0:T(8,128)(2,1)} %param.25) | copy-start | bytes 3145732
  154.9 120.0 %all-gather.10.cloned.1.call-start = ((), (), s32[]{:S(2)}) async-start(), calls=%async_computation.8 | async-start | bytes 2162688 | tf_op jit(solution)/shard_map/all_gather | solution.py:130
  170.5 208.1 %reduce-scatter.3.cloned.1.call-start = ((), (), s32[]{:S(2)}) async-start(), calls=%async_computation.7 | async-start | bytes 2162688 | tf_op jit(solution)/shard_map/reduce_scatter | solution.py:137
  215.2 59.7 %copy-start.10 = (f32[512,256]{1,0:T(8,128)}, f32[512,256]{1,0:T(8,128)S(1)}, u32[]{:S(2)}) copy-start(f32[512,256]{1,0:T(8,128)S(1)} %fusion.19) | copy-start | bytes 1572868
  217.3 267.1 %reduce-scatter.5.cloned.1.call-start = ((), (), s32[]{:S(2)}) async-start(), calls=%async_computation.9 | async-start | bytes 2162688 | tf_op jit(solution)/shard_map/reduce_scatter | solution.py:159
  393.8 105.3 %all-to-all-start.1 = ((bf16[16,2,1024]{2,1,0:T(2,128)(2,1)}), bf16[16,2,1024]{2,1,0:T(2,128)(2,1)S(1)}, u32[]{:S(2)}, u32[]{:S(2)}) async-start(bf16[16,2,1024]{2,1,0:T(2,128)(2,1)} %reshape.206), calls=%async_computation.2 | async-start | bytes 131072 | tf_op jit(solution)/shard_map/all_to_all | solution.py:143
  499.1 23.6 %all-to-all-start.3 = ((bf16[16,2,1024]{2,1,0:T(2,128)(2,1)}), bf16[16,2,1024]{2,1,0:T(2,128)(2,1)S(1)}, u32[]{:S(2)}, u32[]{:S(2)}) async-start(bf16[16,2,1024]{2,1,0:T(2,128)(2,1)} %reshape.208), calls=%async_computation.5 | async-start | bytes 131072 | tf_op jit(solution)/shard_map/all_to_all | solution.py:167
  511.2 96.7 %all-gather.14.cloned.1.call-start = ((), (), s32[]{:S(2)}) async-start(), calls=%async_computation.11 | async-start | bytes 1081344 | tf_op jit(solution)/shard_map/all_gather | solution.py:14
  548.1 3.5 copy-start.8
  548.1 3.5 copy-start.11
  607.9 33.9 %copy-start.2 = (bf16[128,128]{1,0:T(8,128)(2,1)S(1)}, bf16[128,128]{1,0:T(8,128)(2,1)}, u32[]{:S(2)}) copy-start(bf16[128,128]{1,0:T(8,128)(2,1)} %param.18) | copy-start | bytes 98308
Sparse Core Ops, SparseCore 0:
  11.7 63.5 all-gather.11
  155.1 57.7 all-gather.7
  216.6 58.3 all-gather.9
  279.2 99.3 reduce-scatter.2
  382.9 101.5 reduce-scatter.4
  548.2 59.5 all-gather.13
where the time goes:
time: 655 us; the launch traced here: 650 us
  waiting for transfers between devices  379 us (58%)
  blocking collectives  104 us (16%)
  local copies, waits for them, and re-layouts  73.3 us (11%)
  other arithmetic  32.8 us (5%)
  starting transfers between devices  24.5 us (4%)
  matrix products  19.7 us (3%)
  between operations  14.5 us (2%)
    reduce_scatter x1, waiting for transfers between devices, body(): lax.psum_scatter(jnp.dot(row_piece, matrix_down, preferred_element_type=j...  99.2 us
    all_gather x2, waiting for transfers between devices, carried_in(): lax.all_gather(part.astype(kind), axis)  91.5 us
    reduce_scatter x1, waiting for transfers between devices, body(): lax.psum_scatter(lax.dot_general(row_piece, matrix_in, (((1,), (1,)), (()...  78.6 us
    dynamic_slice x128, local copies, waits for them, and re-layouts, step(): part[at].astype(own.dtype)  57.5 us
    all_gather x1, waiting for transfers between devices, body(): lax.all_gather(arrived_cot[0], 'ctx', axis=0, tiled=True)  57.4 us
    all_gather x1, waiting for transfers between devices, body(): lax.all_gather(arrived_rows[0], 'ctx', axis=0, tiled=True)  42.3 us
    psum x1, blocking collectives, body(): square_sum = lax.psum(jnp.sum(mixed_wide * mixed_wide, axis=1), 'exp')  24.8 us
    all_gather x1, blocking collectives, carried_in(): lax.all_gather(part.astype(kind), axis)  24.1 us
  transfers between devices with their start and end apart: 8, of which 7 were waited for; matrix products, arithmetic and copies ran while one was open for 8% of the time, Pallas kernels for 0%

commit v1 on v0

--- a/solution.py
+++ b/solution.py
@@ -6,6 +6,11 @@
 D = 2048
 epsilon = 1e-05
 highest = lax.Precision.HIGHEST
+
+
+def exchange_gather(block, mesh_axis, dim):
+    outgoing = jnp.stack([block] * lax.axis_size(mesh_axis))
+    return jnp.concatenate(lax.all_to_all(outgoing, mesh_axis, 0, 0), axis=dim)
 
 
 def carried_in(value, axis, combine, identity, reverse):
@@ -126,7 +131,7 @@
         lax.all_to_all(spread_cot, "exp", split_axis=0, concat_axis=2, tiled=True),
     )
     expert_rows, cot_rows = (
-        lax.all_gather(arrived_rows[0], "ctx", axis=0, tiled=True),
+        exchange_gather(arrived_rows[0], "ctx", 0),
         lax.all_gather(arrived_cot[0], "ctx", axis=0, tiled=True),
     )
     matrix_in = weight_in[0]

time: 655 us -> 566 us (0.86)
  waiting for transfers between devices: 379 us -> 246 us
  blocking collectives: 104 us -> 130 us
  starting transfers between devices: 24.5 us -> 40.2 us
    all_gather x1, waiting for transfers between devices: 57.4 us -> 0.02 us  [body(): lax.all_gather(arrived_cot[0], 'ctx', axis=0, tiled=True)]
    all_gather x1 -> x0, waiting for transfers between devices: 42.3 us -> none  [body(): lax.all_gather(arrived_rows[0], 'ctx', axis=0, tiled=True)]
    all_to_all x1, blocking collectives: 14.2 us -> 41.4 us  [exchange_gather(): return jnp.concatenate(lax.all_to_all(outgoing, mesh_axis, 0, 0), axis=dim)]
    all_gather x2, waiting for transfers between devices: 91.5 us -> 73.7 us  [carried_in(): lax.all_gather(part.astype(kind), axis)]
    all_to_all x0 -> x1, starting transfers between devices: none -> 15.7 us  [body(): lax.all_to_all(spread_cot, 'exp', split_axis=0, concat_axis=2, tiled=True)]
    reduce_scatter x1, waiting for transfers between devices: 99.2 us -> 84.1 us  [body(): lax.psum_scatter(jnp.dot(row_piece, matrix_down, preferred_element_type=j...]
  transfers between devices with their start and end apart: 8 -> 8, of which waited for: 7 -> 5; matrix products, arithmetic and copies ran while one was open for 8% -> 15% of each run, Pallas kernels for 0% -> 0%
where the time goes in v1:
time: 566 us; the launch traced here: 561 us
  waiting for transfers between devices  246 us (43%)
  blocking collectives  130 us (23%)
  local copies, waits for them, and re-layouts  75.6 us (13%)
  starting transfers between devices  40.2 us (7%)
  other arithmetic  32.8 us (6%)
  matrix products  18.8 us (3%)
  between operations  14.3 us (3%)
    reduce_scatter x1, waiting for transfers between devices, body(): lax.psum_scatter(jnp.dot(row_piece, matrix_down, preferred_element_type=j...  84.1 us
    reduce_scatter x1, waiting for transfers between devices, body(): lax.psum_scatter(lax.dot_general(row_piece, matrix_in, (((1,), (1,)), (()...  78.5 us
    all_gather x2, waiting for transfers between devices, carried_in(): lax.all_gather(part.astype(kind), axis)  73.7 us
    dynamic_slice x128, local copies, waits for them, and re-layouts, step(): part[at].astype(own.dtype)  57.4 us
    all_to_all x1, blocking collectives, exchange_gather(): return jnp.concatenate(lax.all_to_all(outgoing, mesh_axis, 0, 0), axis=dim)  41.4 us
    psum x1, blocking collectives, body(): square_sum = lax.psum(jnp.sum(mixed_wide * mixed_wide, axis=1), 'exp')  25.6 us
    unnamed x4, other arithmetic  23.1 us
    all_gather x1, blocking collectives, carried_in(): lax.all_gather(part.astype(kind), axis)  22.6 us
  transfers between devices with their start and end apart: 8, of which 5 were waited for; matrix products, arithmetic and copies ran while one was open for 15% of the time, Pallas kernels for 0%

profile of v1, /device:TPU:1, one launch (start us, length us, event | category | flops | bytes accessed | tf_op | source)
XLA Modules:
  0.0 560.9 jit_solution(13237454421964409151)
XLA Ops:
  15.5 15.7 %all-to-all-start.3 = ((bf16[16,16,128]{2,1,0:T(8,128)(2,1)}), bf16[16,16,128]{2,1,0:T(8,128)(2,1)S(1)}, u32[]{:S(2)}, u32[]{:S(2)}) async-start(bf16[16,16,128]{2,1,0:T(8,128)(2,1)} %bitcast.24), calls=%async_computation.4 | async-start | bytes 131072 | tf_op jit(solution)/shard_map/all_to_all | solution.py:131
  31.3 22.6 %all-gather.2 = bf16[32,1,4]{2,1,0:T(2,128)(2,1)S(1)} all-gather(bf16[1,1,4]{2,1,0:T(2,128)(2,1)S(1)} %get-tuple-element.356), channel_id=1, replica_groups=mesh['ctx'=32,'exp'=16] {'ctx'}, dimensions={0}, use_global_device_ids=true | all-gather | bytes 264 | tf_op jit(solution)/shard_map/all_gather | solution.py:19
  55.9 19.3 %all-gather.9.cloned.1.call-done = bf16[128,128,32]{1,2,0:T(8,128)(2,1)} async-done(((bf16[4,128,32]{1,2,0:T(8,128)(2,1)}), bf16[128,128,32]{1,2,0:T(8,128)(2,1)}) %all-gather.9.cloned.1.call-update) | async-done | bytes 1048592 | tf_op jit(solution)/shard_map/all_gather | solution.py:19
  75.3 33.7 %while.30 = (s32[]{:T(128)}, f32[4,128,32]{2,1,0:T(8,128)S(1)}, s32[]{:T(128)}, bf16[32,4]{1,0:T(8,128)(2,1)S(1)}, bf16[32,4,128,32]{2,3,1,0:T(8,128)(2,1)}, /*index=5*/s32[]{:T(128)}, s32[]{:T(128)}) while((s32[]{:T(128)}, f32[4,128,32]{2,1,0:T(8,128)S(1)}, s32[]{:T(128)}, bf16[32,4]{1,0:T(8,128)(2,1)S(1)}, ...), condition=%wide.region_2.3_spmd.clone, body=%wide.region_1.2_spmd.clone.sunk | while | flops 81928 | bytes 295065 | solution.py:37
  110.0 25.6 %psum.14 = f32[128]{0:T(128)S(1)} all-reduce(f32[128]{0:T(128)S(1)} %get-tuple-element.351), channel_id=1, replica_groups=mesh['ctx'=32,'exp'=16] {'exp'}, use_global_device_ids=true, to_apply=%region_7.8 | all-reduce | flops 128 | bytes 1024 | tf_op jit(solution)/shard_map/psum | solution.py:103
  136.0 19.0 %all_to_all.68 = bf16[16,16,128]{2,1,0:T(8,128)(2,1)S(1)} all-to-all(bf16[16,16,128]{2,1,0:T(8,128)(2,1)S(1)} %bitcast.191), channel_id=1, replica_groups=mesh['ctx'=32,'exp'=16] {'exp'}, dimensions={0} | all-to-all | bytes 131072 | tf_op jit(solution)/shard_map/all_to_all | solution.py:130
  155.3 41.4 %all_to_all.69 = bf16[32,16,2048]{2,1,0:T(8,128)(2,1)S(1)} all-to-all(bf16[32,16,2048]{2,1,0:T(8,128)(2,1)S(1)} %stack.3), channel_id=1, replica_groups=mesh['ctx'=32,'exp'=16] {'ctx'}, dimensions={0} | all-to-all | bytes 4194304 | tf_op jit(solution)/shard_map/all_to_all | solution.py:13
  198.7 2.1 convolution_convert_fusion.1
  201.1 2.3 fusion.5
  203.4 2.1 convolution_convert_fusion
  205.5 84.1 %reduce-scatter.3.cloned.1.call-done = bf16[16,2048]{1,0:T(8,128)(2,1)} async-done(((bf16[512,2048]{1,0:T(8,128)(2,1)}), bf16[16,2048]{1,0:T(8,128)(2,1)}) %reduce-scatter.3.cloned.1.call-update) | async-done | bytes 65552 | tf_op jit(solution)/shard_map/reduce_scatter | solution.py:142
  289.6 2.0 copy.104
  292.1 11.5 %reduce.3 = bf16[2048,16]{1,0:T(8,128)(2,1)S(1)} reduce(bf16[2048,1,16]{2,1,0:T(2,128)(2,1)S(1)} %bitcast.164, bf16[]{:T(256)} %broadcast.82), dimensions={1}, to_apply=%bitcast.132.reduce_sub_computation | reduce | bytes 131074
  304.8 12.0 %all-to-all-start.2 = ((bf16[16,2,1024]{2,1,0:T(2,128)(2,1)}), bf16[16,2,1024]{2,1,0:T(2,128)(2,1)S(1)}, u32[]{:S(2)}, u32[]{:S(2)}) async-start(bf16[16,2,1024]{2,1,0:T(2,128)(2,1)} %reshape.211), calls=%async_computation.3 | async-start | bytes 131072 | tf_op jit(solution)/shard_map/all_to_all | solution.py:148
  316.9 78.5 %reduce-scatter.5.cloned.1.call-done = bf16[16,2048]{1,0:T(8,128)(2,1)} async-done(((bf16[512,2048]{1,0:T(8,128)(2,1)}), bf16[16,2048]{1,0:T(8,128)(2,1)}) %reduce-scatter.5.cloned.1.call-update) | async-done | bytes 65552 | tf_op jit(solution)/shard_map/reduce_scatter | solution.py:164
  395.4 2.0 copy.110
  397.4 11.5 %reduce.2 = bf16[2048,16]{1,0:T(8,128)(2,1)S(1)} reduce(bf16[2048,1,16]{2,1,0:T(2,128)(2,1)S(1)} %bitcast.165, bf16[]{:T(256)} %broadcast.82), dimensions={1}, to_apply=%bitcast.134.reduce_sub_computation | reduce | bytes 131074
  410.1 12.0 %all-to-all-start.4 = ((bf16[16,2,1024]{2,1,0:T(2,128)(2,1)}), bf16[16,2,1024]{2,1,0:T(2,128)(2,1)S(1)}, u32[]{:S(2)}, u32[]{:S(2)}) async-start(bf16[16,2,1024]{2,1,0:T(2,128)(2,1)} %reshape.213), calls=%async_computation.6 | async-start | bytes 131072 | tf_op jit(solution)/shard_map/all_to_all | solution.py:172
  423.9 9.8 %all-to-all-done.4 = bf16[16,2,1024]{2,1,0:T(2,128)(2,1)S(1)} async-done(((bf16[16,2,1024]{2,1,0:T(2,128)(2,1)}), bf16[16,2,1024]{2,1,0:T(2,128)(2,1)S(1)}, u32[]{:S(2)}, u32[]{:S(2)}) %all-to-all-start.4) | async-done | bytes 65568 | tf_op jit(solution)/shard_map/all_to_all | solution.py:172
  435.7 21.8 %psum.15 = f32[128]{0:T(128)S(1)} all-reduce(f32[128]{0:T(128)S(1)} %fusion.44), channel_id=1, replica_groups=mesh['ctx'=32,'exp'=16] {'exp'}, use_global_device_ids=true, to_apply=%region_13.14 | all-reduce | flops 128 | bytes 1024 | tf_op jit(solution)/shard_map/psum | solution.py:175
  459.2 3.5 fusion.2
  462.6 1.7 fusion.3
  464.4 54.4 %all-gather.11.cloned.1.call-done = bf16[128,128,32]{1,2,0:T(8,128)(2,1)} async-done(((bf16[4,128,32]{1,2,0:T(8,128)(2,1)}), bf16[128,128,32]{1,2,0:T(8,128)(2,1)}) %all-gather.11.cloned.1.call-update) | async-done | bytes 1048592 | tf_op jit(solution)/shard_map/all_gather | solution.py:19
  518.8 34.0 %while.31 = (s32[]{:T(128)}, f32[4,128,32]{2,1,0:T(8,128)S(1)}, s32[]{:T(128)}, bf16[32,4]{1,0:T(8,128)(2,1)S(1)}, bf16[32,4,128,32]{2,3,1,0:T(8,128)(2,1)}, /*index=5*/s32[]{:T(128)}, s32[]{:T(128)}, s32[]{:T(128)}, s32[]{:T(128)}) while((s32[]{:T(128)}, f32[4,128,32]{2,1,0:T(8,128)S(1)}, s32[]{:T(128)}, ...), condition=%wide.region_15.16_spmd.clone, body=%wide.region_14.15_spmd.clone.sunk | while | flops 81932 | bytes 295127 | solution.py:37
  (362 shorter events, 88.9 us)
Async XLA Ops:
  7.2 191.5 %copy-start = (bf16[1,256,2048]{2,1,0:T(8,128)(2,1)S(1)}, bf16[1,256,2048]{2,1,0:T(8,128)(2,1)}, u32[]{:S(2)}) copy-start(bf16[1,256,2048]{2,1,0:T(8,128)(2,1)} %param.26) | copy-start | bytes 3145732
  7.2 68.1 %all-gather.9.cloned.1.call-start = ((), (), s32[]{:S(2)}) async-start(), calls=%async_computation.10 | async-start | bytes 1081344 | tf_op jit(solution)/shard_map/all_gather | solution.py:19
  15.5 39.7 %all-to-all-start.3 = ((bf16[16,16,128]{2,1,0:T(8,128)(2,1)}), bf16[16,16,128]{2,1,0:T(8,128)(2,1)S(1)}, u32[]{:S(2)}, u32[]{:S(2)}) async-start(bf16[16,16,128]{2,1,0:T(8,128)(2,1)} %bitcast.24), calls=%async_computation.4 | async-start | bytes 131072 | tf_op jit(solution)/shard_map/all_to_all | solution.py:131
  31.2 169.8 %all-gather.7.cloned.1.call-start = ((), (), s32[]{:S(2)}) async-start(), calls=%async_computation.8 | async-start | bytes 2162688 | tf_op jit(solution)/shard_map/all_gather | solution.py:135
  55.9 233.7 %reduce-scatter.3.cloned.1.call-start = ((), (), s32[]{:S(2)}) async-start(), calls=%async_computation.7 | async-start | bytes 2162688 | tf_op jit(solution)/shard_map/reduce_scatter | solution.py:142
  75.2 33.7 %copy-start.4 = (bf16[128,128]{1,0:T(8,128)(2,1)S(1)}, bf16[128,128]{1,0:T(8,128)(2,1)}, u32[]{:S(2)}) copy-start(bf16[128,128]{1,0:T(8,128)(2,1)} %param.19) | copy-start | bytes 98308
  75.2 34.1 %copy-start.10 = (f32[4]{0:T(128)S(1)}, f32[4]{0:T(128)}, u32[]{:S(2)}) copy-start(f32[4]{0:T(128)} %param.21) | copy-start | bytes 52
  75.2 34.7 %copy-start.6 = (bf16[128,128]{1,0:T(8,128)(2,1)S(1)}, bf16[128,128]{1,0:T(8,128)(2,1)}, u32[]{:S(2)}) copy-start(bf16[128,128]{1,0:T(8,128)(2,1)} %param.16) | copy-start | bytes 98308
  75.3 60.4 %copy-start.7 = (f32[128]{0:T(128)S(1)}, f32[128]{0:T(128)}, u32[]{:S(2)}) copy-start(f32[128]{0:T(128)} %param.22) | copy-start | bytes 1540
  155.3 42.7 %copy-start.2 = (bf16[1,2048,256]{2,1,0:T(8,128)(2,1)S(1)}, bf16[1,2048,256]{2,1,0:T(8,128)(2,1)}, u32[]{:S(2)}) copy-start(bf16[1,2048,256]{2,1,0:T(8,128)(2,1)} %param.25) | copy-start | bytes 3145732
  196.6 1.3 copy-start.1
  198.7 2.4 copy-start.11
  200.8 194.6 %reduce-scatter.5.cloned.1.call-start = ((), (), s32[]{:S(2)}) async-start(), calls=%async_computation.9 | async-start | bytes 2162688 | tf_op jit(solution)/shard_map/reduce_scatter | solution.py:164
  304.8 105.3 %all-to-all-start.2 = ((bf16[16,2,1024]{2,1,0:T(2,128)(2,1)}), bf16[16,2,1024]{2,1,0:T(2,128)(2,1)S(1)}, u32[]{:S(2)}, u32[]{:S(2)}) async-start(bf16[16,2,1024]{2,1,0:T(2,128)(2,1)} %reshape.211), calls=%async_computation.3 | async-start | bytes 131072 | tf_op jit(solution)/shard_map/all_to_all | solution.py:148
  410.1 23.6 %all-to-all-start.4 = ((bf16[16,2,1024]{2,1,0:T(2,128)(2,1)}), bf16[16,2,1024]{2,1,0:T(2,128)(2,1)S(1)}, u32[]{:S(2)}, u32[]{:S(2)}) async-start(bf16[16,2,1024]{2,1,0:T(2,128)(2,1)} %reshape.213), calls=%async_computation.6 | async-start | bytes 131072 | tf_op jit(solution)/shard_map/all_to_all | solution.py:172
  422.2 96.6 %all-gather.11.cloned.1.call-start = ((), (), s32[]{:S(2)}) async-start(), calls=%async_computation.11 | async-start | bytes 1081344 | tf_op jit(solution)/shard_map/all_gather | solution.py:19
  423.3 11.9 %copy-start.8 = (f32[128,2]{0,1:T(2,128)S(1)}, f32[128,2]{0,1:T(2,128)}, u32[]{:S(2)}) copy-start(f32[128,2]{0,1:T(2,128)} %param.23) | copy-start | bytes 3076
  423.9 33.6 %copy-start.5 = (bf16[128,128]{1,0:T(8,128)(2,1)S(1)}, bf16[128,128]{1,0:T(8,128)(2,1)}, u32[]{:S(2)}) copy-start(bf16[128,128]{1,0:T(8,128)(2,1)} %param.27) | copy-start | bytes 98308
  459.1 3.5 copy-start.9
  459.1 3.5 copy-start.12
  518.8 34.0 %copy-start.3 = (bf16[128,128]{1,0:T(8,128)(2,1)S(1)}, bf16[128,128]{1,0:T(8,128)(2,1)}, u32[]{:S(2)}) copy-start(bf16[128,128]{1,0:T(8,128)(2,1)} %param.18) | copy-start | bytes 98308
Sparse Core Ops, SparseCore 0:
  11.7 63.5 all-gather.8
  79.0 58.4 all-gather.6
  200.9 88.6 reduce-scatter.2
  293.9 101.4 reduce-scatter.4
  459.2 59.5 all-gather.10
